TPU v7x, 32 devices: a whole 2x2x4 slice. The times are simulated.
32 devices in a mesh: fsdp: 4 (over y, x), rep: 8 (over z, core).
Axes of the slice: x: 2, y: 2, z: 4, core: 2. Of those that a mesh axis runs over, the one named last changes fastest.
Arguments:
- tokens: bfloat16 [64, 256, 384], P(('fsdp', 'rep')), may hold values from -6 to 6
- conditions: bfloat16 [64, 384], P(('fsdp', 'rep')), may hold values from -6 to 6
- assignment: int32 [64], P(('fsdp', 'rep')), may hold values from 0 to 63, each once
- params: float32 [2654208], P('fsdp')
- momentum: float32 [2654208], P('fsdp'), may hold values from -24 to 24
- cotangent: bfloat16 [64, 256, 384], P(('fsdp', 'rep')), may hold values from -6 to 6
Outputs:
- blended: bfloat16 [64, 256, 384], P(('fsdp', 'rep'))
- grad_tokens: float32 [64, 256, 384], P(('fsdp', 'rep'))
- grad_params: float32 [2654208], P('fsdp')
- new_params: float32 [2654208], P('fsdp')
- new_momentum: float32 [2654208], P('fsdp')
Inputs may be any that keep to these rules, and one draw needn't show every extreme that they name: assignment is a permutation of the latent numbers.
All inputs are finite; a program needn't handle non-finite values.
Results may differ from a plain program's by a relative error of at most 0.014.
The roundings to bfloat16 on the way count: a program that leaves them out, or rounds other values in their place, can miss the bound.
Values may be sent and summed in bfloat16 or wider, within the bound.
No kernel may reach another device: no remote copies, remote signals or barrier semaphores. Data moves between devices by JAX's collectives and lax.ppermute only.
A program may use at most 192 MiB of HBM per device.

v0:
```python
import math
import jax
import jax.numpy as jnp
from jax import lax
from jax.sharding import PartitionSpec as P

D = 384
HEADS = 6
HD = 64
FF = 1536
SEQ = 256
NS_ITERS = 3
LN_EPSILON = 1e-06
MOMENTUM_RATE = 0.95
LEARN_RATE = 0.2
COEFF_A = 3.4445
COEFF_B = -4.775
COEFF_C = 2.0315


def matrix_shapes():
    return [(D, 6 * D), (D, 3 * D), (D, D), (D, FF), (FF, D)]


def unpack(flat_vec):
    pieces = []
    offset = 0
    for rows_count, cols_count in matrix_shapes():
        pieces.append(
            flat_vec[offset : offset + rows_count * cols_count].reshape(rows_count, cols_count)
        )
        offset += rows_count * cols_count
    return pieces


def matmul(lhs_array, rhs_array):
    return jnp.dot(lhs_array, rhs_array, preferred_element_type=jnp.float32)


def contract(pattern, lhs_array, rhs_array):
    return jnp.einsum(pattern, lhs_array, rhs_array, preferred_element_type=jnp.float32)


def modulate(hidden, shifts, scales):
    center = jnp.mean(hidden, axis=-1, keepdims=True)
    spread = jnp.mean(jnp.square(hidden - center), axis=-1, keepdims=True)
    return (hidden - center) * lax.rsqrt(spread + LN_EPSILON) * (1.0 + scales) + shifts


def gelu_tanh(values_in):
    return jax.nn.gelu(values_in, approximate=True)


def orthogonalize(matrix):
    flipped = matrix.shape[0] > matrix.shape[1]
    current = matrix.T if flipped else matrix
    current = current / (jnp.sqrt(jnp.sum(current * current)) + 1e-07)
    for newton_step in range(NS_ITERS):
        square = jnp.dot(current, current.T, precision=lax.Precision.HIGHEST)
        polynomial = COEFF_B * square + COEFF_C * jnp.dot(
            square, square, precision=lax.Precision.HIGHEST
        )
        current = COEFF_A * current + jnp.dot(polynomial, current, precision=lax.Precision.HIGHEST)
    return current.T if flipped else current


def update_scale(rows_count, cols_count):
    return LEARN_RATE * 0.2 * math.sqrt(max(rows_count, cols_count))


def scaled_update(matrix, factor):
    return (factor * orthogonalize(matrix)).reshape(-1)


def empty_update(matrix, factor):
    return jnp.zeros((matrix.shape[0] * matrix.shape[1],), jnp.float32)


def forward_pass(tokens, cond_rows, weights):
    adaln_weight, qkv_weight, out_weight, up_weight, down_weight = weights
    batch_size = tokens.shape[0]
    row_count = batch_size * SEQ
    silu_cond = jax.nn.silu(cond_rows.astype(jnp.float32)).astype(jnp.bfloat16)
    modulation = matmul(silu_cond, adaln_weight).reshape(batch_size, 6, 1, D)
    mod_parts = tuple((modulation[:, position] for position in range(6)))
    shift_attn, scale_attn, gate_attn, shift_mlp, scale_mlp, gate_mlp = mod_parts
    residual = tokens.astype(jnp.float32)
    attn_input = modulate(residual, shift_attn, scale_attn).astype(jnp.bfloat16)
    qkv_all = matmul(attn_input.reshape(row_count, D), qkv_weight).astype(jnp.bfloat16)
    qkv_heads = qkv_all.reshape(batch_size, SEQ, 3, HEADS, HD).transpose(2, 0, 3, 1, 4)
    queries, key_vecs, value_vecs = (qkv_heads[0], qkv_heads[1], qkv_heads[2])
    scores = contract("bhqd,bhkd->bhqk", queries, key_vecs) * HD ** (-0.5)
    log_total = jax.nn.logsumexp(scores, axis=-1, keepdims=True)
    attn_probs = jnp.exp(scores - log_total).astype(jnp.bfloat16)
    attn_mixed = contract("bhqk,bhkd->bhqd", attn_probs, value_vecs).astype(jnp.bfloat16)
    attn_mixed = attn_mixed.transpose(0, 2, 1, 3).reshape(row_count, D)
    attn_out = matmul(attn_mixed, out_weight).reshape(batch_size, SEQ, D)
    after_attn = residual + gate_attn * attn_out
    mlp_input = (
        modulate(after_attn, shift_mlp, scale_mlp).astype(jnp.bfloat16).reshape(row_count, D)
    )
    pre_act = matmul(mlp_input, up_weight)
    activated = gelu_tanh(pre_act).astype(jnp.bfloat16)
    mlp_out = matmul(activated, down_weight).reshape(batch_size, SEQ, D)
    blended = (after_attn + gate_mlp * mlp_out).astype(jnp.bfloat16)
    kept_state = (
        silu_cond,
        mod_parts,
        residual,
        attn_input,
        queries,
        key_vecs,
        value_vecs,
        log_total,
        attn_mixed,
        attn_out,
        after_attn,
        mlp_input,
        pre_act,
        activated,
        mlp_out,
    )
    return (blended, kept_state)


def backward_pass(kept_state, weights, cotangent):
    (
        silu_cond,
        mod_parts,
        residual,
        attn_input,
        queries,
        key_vecs,
        value_vecs,
        log_total,
        attn_mixed,
        attn_out,
        after_attn,
        mlp_input,
        pre_act,
        activated,
        mlp_out,
    ) = kept_state
    adaln_weight, qkv_weight, out_weight, up_weight, down_weight = weights
    shift_attn, scale_attn, gate_attn, shift_mlp, scale_mlp, gate_mlp = mod_parts
    batch_size = cotangent.shape[0]
    row_count = batch_size * SEQ
    upstream = cotangent.astype(jnp.float32)
    grad_gate_mlp = jnp.sum(upstream * mlp_out, axis=1, keepdims=True)
    grad_mlp_out = (upstream * gate_mlp).astype(jnp.bfloat16).reshape(row_count, D)
    grad_down = matmul(activated.T, grad_mlp_out)
    grad_act = matmul(grad_mlp_out, down_weight.T)
    grad_pre = jax.vjp(gelu_tanh, pre_act)[1](grad_act)[0].astype(jnp.bfloat16)
    grad_up = matmul(mlp_input.T, grad_pre)
    grad_mlp_in = matmul(grad_pre, up_weight.T).reshape(batch_size, SEQ, D)
    grad_after, grad_shift_mlp, grad_scale_mlp = jax.vjp(
        modulate, after_attn, shift_mlp, scale_mlp
    )[1](grad_mlp_in)
    grad_after = upstream + grad_after
    grad_gate_attn = jnp.sum(grad_after * attn_out, axis=1, keepdims=True)
    grad_attn_out = (grad_after * gate_attn).astype(jnp.bfloat16).reshape(row_count, D)
    grad_outw = matmul(attn_mixed.T, grad_attn_out)
    grad_mixed = matmul(grad_attn_out, out_weight.T).astype(jnp.bfloat16)
    grad_mixed = grad_mixed.reshape(batch_size, SEQ, HEADS, HD).transpose(0, 2, 1, 3)
    scores = contract("bhqd,bhkd->bhqk", queries, key_vecs) * HD ** (-0.5)
    probs_full = jnp.exp(scores - log_total)
    grad_values = contract("bhqk,bhqd->bhkd", probs_full.astype(jnp.bfloat16), grad_mixed)
    grad_probs = contract("bhqd,bhkd->bhqk", grad_mixed, value_vecs)
    row_dots = jnp.sum(probs_full * grad_probs, axis=-1, keepdims=True)
    grad_scores = (probs_full * (grad_probs - row_dots) * HD ** (-0.5)).astype(jnp.bfloat16)
    grad_queries = contract("bhqk,bhkd->bhqd", grad_scores, key_vecs)
    grad_keys = contract("bhqk,bhqd->bhkd", grad_scores, queries)
    grad_qkv = jnp.stack([grad_queries, grad_keys, grad_values], axis=0).transpose(1, 3, 0, 2, 4)
    grad_qkv = grad_qkv.reshape(row_count, 3 * D).astype(jnp.bfloat16)
    grad_qkvw = matmul(attn_input.reshape(row_count, D).T, grad_qkv)
    grad_attn_in = matmul(grad_qkv, qkv_weight.T).reshape(batch_size, SEQ, D)
    grad_resid, grad_shift_attn, grad_scale_attn = jax.vjp(
        modulate, residual, shift_attn, scale_attn
    )[1](grad_attn_in)
    grad_tokens = grad_after + grad_resid
    grad_mod = jnp.concatenate(
        [
            grad_shift_attn,
            grad_scale_attn,
            grad_gate_attn,
            grad_shift_mlp,
            grad_scale_mlp,
            grad_gate_mlp,
        ],
        axis=1,
    )
    grad_mod = grad_mod.reshape(batch_size, 6 * D).astype(jnp.bfloat16)
    grad_adaln = matmul(silu_cond.T, grad_mod)
    flat_grads = jnp.concatenate(
        [
            grad_adaln.reshape(-1),
            grad_qkvw.reshape(-1),
            grad_outw.reshape(-1),
            grad_up.reshape(-1),
            grad_down.reshape(-1),
        ]
    )
    return (grad_tokens, flat_grads)


def on_device(tokens, conditions, assignment, params, momentum, cotangent):
    cond_table = lax.all_gather(conditions, ("fsdp", "rep"), axis=0, tiled=True)
    cond_rows = jnp.take(cond_table, assignment, axis=0)
    low_params = params.astype(jnp.bfloat16)
    gathered = lax.all_gather(low_params, "fsdp", axis=0, tiled=True)
    blended, kept_state = forward_pass(tokens, cond_rows, unpack(gathered))
    back_flat = lax.all_gather(low_params, "fsdp", axis=0, tiled=True)
    grad_tokens, flat_grads = backward_pass(kept_state, unpack(back_flat), cotangent)
    group_part = lax.psum_scatter(flat_grads, "fsdp", scatter_dimension=0, tiled=True)
    full_grad = lax.psum(group_part, "rep")
    new_momentum = MOMENTUM_RATE * momentum + full_grad
    whole_mom = lax.all_gather(new_momentum, "fsdp", axis=0, tiled=True)
    fsdp_rank = lax.axis_index("fsdp")
    group_size = lax.axis_size("fsdp")
    shard_len = params.shape[0]
    updates = []
    offset = 0
    for rows_count, cols_count in matrix_shapes():
        length = rows_count * cols_count
        piece = whole_mom[offset : offset + length].reshape(rows_count, cols_count)
        factor = jnp.float32(update_scale(rows_count, cols_count))
        owner_rank = (offset // shard_len + group_size // 2) % group_size
        updates.append(
            lax.cond(fsdp_rank == owner_rank, scaled_update, empty_update, piece, factor)
        )
        offset += length
    local_update = lax.psum_scatter(
        jnp.concatenate(updates), "fsdp", scatter_dimension=0, tiled=True
    )
    new_params = params - local_update
    return (blended, grad_tokens, full_grad, new_params, new_momentum)


def solution(mesh):
    in_specs = (
        P(("fsdp", "rep"), None, None),
        P(("fsdp", "rep"), None),
        P(("fsdp", "rep")),
        P("fsdp"),
        P("fsdp"),
        P(("fsdp", "rep"), None, None),
    )
    out_specs = (
        P(("fsdp", "rep"), None, None),
        P(("fsdp", "rep"), None, None),
        P("fsdp"),
        P("fsdp"),
        P("fsdp"),
    )
    return jax.shard_map(
        on_device, mesh=mesh, in_specs=in_specs, out_specs=out_specs, check_vma=False
    )
```

profile of v0, /device:TPU:0, one launch (start us, length us, event | category | flops | bytes accessed | tf_op | source)
XLA Modules:
  0.0 911.6 jit_solution(14796318998570174122)
XLA Ops:
  7.2 3.0 convert_element_type.90
  10.3 44.1 %all-gather = bf16[32,2,384]{2,1,0:T(2,128)(2,1)S(1)} all-gather(bf16[1,2,384]{2,1,0:T(2,128)(2,1)S(1)} %bitcast.245), channel_id=1, replica_groups=mesh['fsdp'=4,'rep'=8] {'fsdp','rep'}, dimensions={0}, use_global_device_ids=true | all-gather | bytes 50688 | tf_op jit(solution)/shard_map/all_gather | solution.py:207
  55.5 19.7 %all-gather.4.cloned.1.call-done = bf16[2654208]{0:T(1024)(128)(2,1)} async-done(((bf16[663552]{0:T(1024)(128)(2,1)}), bf16[2654208]{0:T(1024)(128)(2,1)}) %all-gather.4.cloned.1.call-update) | async-done | bytes 5308432 | tf_op jit(solution)/shard_map/all_gather | solution.py:210
  79.1 2.0 reshape.358
  81.1 2.0 slice.162
  88.2 2.2 reshape.357
  90.4 2.2 slice.172
  92.5 3.0 slice.157
  95.5 2.8 copy.42
  99.5 2.1 fusion.67
  108.5 2.8 fusion.36
  111.2 2.2 fusion.116
  115.5 2.4 fusion.117
  118.0 2.5 fusion.72
  123.3 1.9 copy.47
  127.1 2.5 convolution_bitcast_fusion
  129.6 3.3 fusion.73
  132.9 5.2 fusion.49
  138.1 5.1 fusion.52
  144.6 2.3 copy.55
  153.1 3.4 reshape.341
  158.1 2.5 fusion.68
  164.9 2.1 reshape.337
  167.0 4.1 constant_dynamic-update-slice_fusion.6
  179.8 205.9 %all-reduce.8.cloned.1.call-done = f32[2654208]{0:T(1024)} async-done(((f32[2654208]{0:T(1024)}), f32[2654208]{0:T(1024)}) %all-reduce.8.cloned.1.call-update) | async-done | bytes 10616848
  385.8 3.4 dynamic-slice.1
  389.3 69.3 %all-reduce.6.cloned.1.call-done = f32[663552]{0:T(1024)} async-done(((f32[663552]{0:T(1024)}), f32[663552]{0:T(1024)}) %all-reduce.6.cloned.1.call-update) | async-done | bytes 2654224 | tf_op jit(solution)/shard_map/psum | solution.py:215
  458.5 3.6 multiply_add_fusion.3
  462.2 105.5 %all-gather.6.cloned.1.call-done = f32[2654208]{0:T(1024)} async-done(((f32[663552]{0:T(1024)}), f32[2654208]{0:T(1024)}) %all-gather.6.cloned.1.call-update) | async-done | bytes 10616848 | tf_op jit(solution)/shard_map/all_gather | solution.py:217
  567.7 9.3 %conditional.5 = (f32[884736]{0:T(1024)S(1)}) conditional(s32[]{:T(128)} %convert_element_type.110, () %tuple.38, f32[2654208]{0:T(1024)} %all-gather.6.cloned.1.call-done), branch_computations={%region_21.22_spmd, %region_22.24_spmd} | conditional | flops 26509787136 | bytes 63701028 | solution.py:229
  577.0 2.1 constant_dynamic-update-slice_fusion.7
  579.1 14.8 %conditional.6 = (f32[442368]{0:T(1024)S(1)}) conditional(s32[]{:T(128)} %convert_element_type.111, () %tuple.39, f32[2654208]{0:T(1024)} %all-gather.6.cloned.1.call-done), branch_computations={%region_24.25_spmd, %region_25.27_spmd} | conditional | flops 14274772992 | bytes 35389476 | solution.py:229
  595.3 15.7 %conditional.7 = (f32[147456]{0:T(1024)S(1)}) conditional(s32[]{:T(128)} %convert_element_type.112, () %tuple.40, f32[2654208]{0:T(1024)} %all-gather.6.cloned.1.call-done), branch_computations={%region_27.28_spmd, %region_28.30_spmd} | conditional | flops 6118096896 | bytes 16515108 | solution.py:229
  611.8 41.5 %conditional.8 = (f32[589824]{0:T(1024)S(1)}) conditional(s32[]{:T(128)} %convert_element_type.112, () %tuple.41, f32[2654208]{0:T(1024)} %all-gather.6.cloned.1.call-done), branch_computations={%region_30.31_spmd, %region_31.33_spmd} | conditional | flops 18353111040 | bytes 44826660 | solution.py:229
  611.8 2.9 multiply_reduce_fusion.3
  615.4 3.2 slice_divide_fusion.3
  618.6 2.4 div.75
  621.1 4.0 fusion.109
  626.3 4.0 convolution_add_fusion.11
  630.3 4.2 fusion.110
  635.8 4.0 convolution_add_fusion.10
  639.8 4.0 fusion.111
  645.1 5.5 fusion.12
  650.6 2.3 reshape.307
  655.0 10.3 %conditional.9 = (f32[589824]{0:T(1024)S(1)}) conditional(s32[]{:T(128)} %convert_element_type.113, () %tuple.42, f32[2654208]{0:T(1024)} %all-gather.6.cloned.1.call-done), branch_computations={%region_33.34_spmd, %region_34.36_spmd} | conditional | flops 18360188928 | bytes 110887024 | solution.py:229
  668.1 2.6 fusion.65
  670.7 228.7 %all-reduce.10.cloned.1.call-done = f32[2654208]{0:T(1024)} async-done(((f32[2654208]{0:T(1024)}), f32[2654208]{0:T(1024)}) %all-reduce.10.cloned.1.call-update) | async-done | bytes 10616848
  899.5 3.7 dynamic-slice_subtract_fusion
  (215 shorter events, 73.5 us)
Async XLA Ops:
  7.2 3.1 copy-start.55
  7.2 47.2 %copy-start.58 = (s32[2]{0:T(128)S(1)}, s32[2]{0:T(128)}, u32[]{:S(2)}) copy-start(s32[2]{0:T(128)} %param.18) | copy-start | bytes 28
  7.2 47.8 %copy-start.3 = (bf16[2,256,384]{2,1,0:T(8,128)(2,1)S(1)}, bf16[2,256,384]{2,1,0:T(8,128)(2,1)}, u32[]{:S(2)}) copy-start(bf16[2,256,384]{2,1,0:T(8,128)(2,1)} %param.16) | copy-start | bytes 1179652
  7.2 68.0 %all-gather.4.cloned.1.call-start = ((), (), s32[]{:S(2)}) async-start(), calls=%async_computation | async-start | bytes 6635520 | tf_op jit(solution)/shard_map/all_gather | solution.py:210
  10.3 375.5 %all-reduce.8.cloned.1.call-start = ((), (), s32[]{:S(2)}) async-start(), calls=%async_computation.3 | async-start | bytes 21233664
  55.0 43.3 %copy-start.46 = (bf16[2,384]{1,0:T(2,128)(2,1)}, bf16[2,384]{1,0:T(2,128)(2,1)S(1)}, u32[]{:S(2)}) copy-start(bf16[2,384]{1,0:T(2,128)(2,1)S(1)} %gather_fusion) | copy-start | bytes 4612
  55.2 44.3 %copy-start.34 = (f32[2,256]{1,0:T(2,128)}, f32[2,256]{1,0:T(2,128)S(1)}, u32[]{:S(2)}) copy-start(f32[2,256]{1,0:T(2,128)S(1)} %broadcast_multiply_fusion.2) | copy-start | bytes 6148
  55.5 25.6 %copy-start.42 = (f32[2,256]{1,0:T(2,128)}, f32[2,256]{1,0:T(2,128)S(1)}, u32[]{:S(2)}) copy-start(f32[2,256]{1,0:T(2,128)S(1)} %fusion.69) | copy-start | bytes 6148
  55.5 42.8 %copy-start.52 = (pred[2]{0:T(512)(128)(4,1)}, pred[2]{0:T(512)(128)(4,1)S(1)}, u32[]{:S(2)}) copy-start(pred[2]{0:T(512)(128)(4,1)S(1)} %compare_and_fusion) | copy-start | bytes 10
  55.5 44.0 %copy-start.44 = (f32[2,256]{1,0:T(2,128)}, f32[2,256]{1,0:T(2,128)S(1)}, u32[]{:S(2)}) copy-start(f32[2,256]{1,0:T(2,128)S(1)} %fusion.85) | copy-start | bytes 6148
  90.3 2.2 slice-start
  98.2 3.3 copy-start.15
  99.5 3.5 copy-start.37
  99.5 3.5 copy-start.39
  101.6 1.5 copy-start.16
  105.5 2.9 copy-start.20
  105.5 1.4 copy-start.30
  107.0 1.5 copy-start.26
  107.0 1.5 copy-start.29
  111.2 2.2 copy-start.28
  115.5 2.5 copy-start.14
  115.5 2.5 copy-start.25
  115.5 2.4 copy-start.38
  118.0 4.2 copy-start.32
  127.1 2.5 copy-start.22
  144.6 3.4 copy-start.21
  146.9 1.6 copy-start.19
  148.0 3.6 copy-start.2
  153.1 3.5 copy-start.13
  156.6 1.5 copy-start.33
  156.6 1.5 copy-start.35
  156.6 1.5 copy-start.40
  156.6 1.5 copy-start.45
  158.1 2.5 copy-start.17
  161.4 1.4 copy-start.51
  161.4 1.4 copy-start.57
  161.4 1.4 copy-start.56
  161.4 1.4 copy-start.50
  161.4 2.0 copy-start.47
  167.0 4.1 copy-start.10
  171.1 2.7 copy-start.8
  173.8 2.5 copy-start.7
  178.0 280.6 %all-reduce.6.cloned.1.call-start = ((), (), s32[]{:S(2)}) async-start(), calls=%async_computation.1 | async-start | bytes 5308416 | tf_op jit(solution)/shard_map/psum | solution.py:215
  389.2 69.3 %copy-start.23 = (f32[663552]{0:T(1024)S(1)}, f32[663552]{0:T(1024)}, u32[]{:S(2)}) copy-start(f32[663552]{0:T(1024)} %param.20) | copy-start | bytes 7962628
  389.2 178.5 %all-gather.6.cloned.1.call-start = ((), (), s32[]{:S(2)}) async-start(), calls=%async_computation.2 | async-start | bytes 13271040 | tf_op jit(solution)/shard_map/all_gather | solution.py:217
  462.1 437.3 %all-reduce.10.cloned.1.call-start = ((), (), s32[]{:S(2)}) async-start(), calls=%async_computation.4 | async-start | bytes 21233664
  666.8 232.6 %copy-start.5 = (f32[663552]{0:T(1024)S(1)}, f32[663552]{0:T(1024)}, u32[]{:S(2)}) copy-start(f32[663552]{0:T(1024)} %param.19) | copy-start | bytes 7962628
  899.5 3.7 copy-start.6
  (15 other events, 14.5 us)
Sparse Core Ops, SparseCore 0:
  10.4 64.7 all-gather.3
  178.1 207.6 all-reduce.7
  389.3 69.1 all-reduce.5
  462.2 105.4 all-gather.5
  667.0 232.4 all-reduce.9
where the time goes:
time: 916 us; the launch traced here: 912 us
  waiting for transfers between devices  629 us (69%)
  matrix products  80.4 us (9%)
  local copies, waits for them, and re-layouts  77.9 us (9%)
  blocking collectives  44.1 us (5%)
  loops' own time  36.2 us (4%)
  other arithmetic  28.1 us (3%)
  between operations  15.4 us (2%)
    unnamed x7, waiting for transfers between devices  435 us
    all_gather x1, waiting for transfers between devices, on_device(): whole_mom = lax.all_gather(new_momentum, 'fsdp', axis=0, tiled=True)  106 us
    psum x1, waiting for transfers between devices, on_device(): full_grad = lax.psum(group_part, 'rep')  69.3 us
    all_gather x1, blocking collectives, on_device(): cond_table = lax.all_gather(conditions, ('fsdp', 'rep'), axis=0, tiled=True)  44.1 us
    another operation x5, loops' own time, on_device(): lax.cond(fsdp_rank == owner_rank, scaled_update, empty_update, piece, fac...  36.2 us
    unnamed x133, local copies, waits for them, and re-layouts  26.7 us
    dot_general x14, matrix products, matmul(): return jnp.dot(lhs_array, rhs_array, preferred_element_type=jnp.float32)  22 us
    slice x14, local copies, waits for them, and re-layouts, unpack(): flat_vec[offset:offset + rows_count * cols_count]  20.3 us
  transfers between devices with their start and end apart: 5, of which 5 were waited for; matrix products, arithmetic and copies ran while one was open for 0% of the time, Pallas kernels for 0%

commit v1 on v0

--- a/solution.py
+++ b/solution.py
@@ -16,6 +16,15 @@
 COEFF_A = 3.4445
 COEFF_B = -4.775
 COEFF_C = 2.0315
+
+
+def supply_patch_for(which_axis, z_in):
+    world_n = lax.axis_size(which_axis)
+    step_out = lambda oldest: [(j, j ^ oldest) for j in range(world_n)]
+    v_next = z_in
+    for idx in range(world_n.bit_length() - 1):
+        v_next = v_next + lax.ppermute(v_next, axis_name=which_axis, perm=step_out(1 << idx))
+    return v_next
 
 
 def matrix_shapes():
@@ -212,7 +221,7 @@
     back_flat = lax.all_gather(low_params, "fsdp", axis=0, tiled=True)
     grad_tokens, flat_grads = backward_pass(kept_state, unpack(back_flat), cotangent)
     group_part = lax.psum_scatter(flat_grads, "fsdp", scatter_dimension=0, tiled=True)
-    full_grad = lax.psum(group_part, "rep")
+    full_grad = supply_patch_for("rep", z_in=group_part)
     new_momentum = MOMENTUM_RATE * momentum + full_grad
     whole_mom = lax.all_gather(new_momentum, "fsdp", axis=0, tiled=True)
     fsdp_rank = lax.axis_index("fsdp")

time: 916 us -> 1030 us (1.12)
  waiting for transfers between devices: 629 us -> 738 us
    ppermute x0 -> x3, waiting for transfers between devices: none -> 177 us  [supply_patch_for(): lax.ppermute(v_next, axis_name=which_axis, perm=step_out(1 << idx))]
    psum x1 -> x0, waiting for transfers between devices: 69.3 us -> none  [on_device(): full_grad = lax.psum(group_part, 'rep')]
    unnamed x133 -> x130, local copies, waits for them, and re-layouts: 26.7 us -> 23.5 us
    unnamed x7 -> x6, waiting for transfers between devices: 435 us -> 435 us
  transfers between devices with their start and end apart: 5 -> 7, of which waited for: 5 -> 7; matrix products, arithmetic and copies ran while one was open for 0% -> 0% of each run, Pallas kernels for 0% -> 0%
where the time goes in v1:
time: 1030 us; the launch traced here: 1020 us
  waiting for transfers between devices  738 us (72%)
  matrix products  80.4 us (8%)
  local copies, waits for them, and re-layouts  74.7 us (7%)
  blocking collectives  44.1 us (4%)
  loops' own time  36.1 us (4%)
  other arithmetic  29.5 us (3%)
  between operations  15.4 us (1%)
    unnamed x6, waiting for transfers between devices  435 us
    ppermute x3, waiting for transfers between devices, supply_patch_for(): lax.ppermute(v_next, axis_name=which_axis, perm=step_out(1 << idx))  177 us
    all_gather x1, waiting for transfers between devices, on_device(): whole_mom = lax.all_gather(new_momentum, 'fsdp', axis=0, tiled=True)  106 us
    all_gather x1, blocking collectives, on_device(): cond_table = lax.all_gather(conditions, ('fsdp', 'rep'), axis=0, tiled=True)  44.1 us
    another operation x5, loops' own time, on_device(): lax.cond(fsdp_rank == owner_rank, scaled_update, empty_update, piece, fac...  36.1 us
    unnamed x130, local copies, waits for them, and re-layouts  23.5 us
    dot_general x14, matrix products, matmul(): return jnp.dot(lhs_array, rhs_array, preferred_element_type=jnp.float32)  22.1 us
  transfers between devices with their start and end apart: 7, of which 7 were waited for; matrix products, arithmetic and copies ran while one was open for 0% of the time, Pallas kernels for 0%

profile of v1, /device:TPU:0, one launch (start us, length us, event | category | flops | bytes accessed | tf_op | source)
XLA Modules:
  0.0 1022.4 jit_solution(5635797342942901850)
XLA Ops:
  7.2 3.0 convert_element_type.90
  10.3 44.1 %all-gather = bf16[32,2,384]{2,1,0:T(2,128)(2,1)S(1)} all-gather(bf16[1,2,384]{2,1,0:T(2,128)(2,1)S(1)} %bitcast.245), channel_id=1, replica_groups=mesh['fsdp'=4,'rep'=8] {'fsdp','rep'}, dimensions={0}, use_global_device_ids=true | all-gather | bytes 50688 | tf_op jit(solution)/shard_map/all_gather | solution.py:216
  55.5 19.7 %all-gather.4.cloned.1.call-done = bf16[2654208]{0:T(1024)(128)(2,1)} async-done(((bf16[663552]{0:T(1024)(128)(2,1)}), bf16[2654208]{0:T(1024)(128)(2,1)}) %all-gather.4.cloned.1.call-update) | async-done | bytes 5308432 | tf_op jit(solution)/shard_map/all_gather | solution.py:219
  81.1 2.0 slice.162
  88.2 2.1 reshape.357
  90.4 2.2 slice.172
  92.5 3.0 slice.157
  95.5 2.8 copy.42
  99.5 2.1 fusion.67
  108.5 2.8 fusion.36
  111.2 2.2 fusion.116
  115.6 2.4 fusion.117
  118.0 2.5 fusion.72
  127.1 2.5 convolution_bitcast_fusion
  129.6 3.2 fusion.73
  132.9 5.2 fusion.49
  138.1 5.1 fusion.52
  144.6 2.2 copy.55
  153.1 3.4 reshape.341
  158.1 2.5 fusion.68
  164.9 2.1 reshape.337
  167.0 4.1 constant_dynamic-update-slice_fusion.6
  179.8 206.0 %all-reduce.5.cloned.1.call-done = f32[2654208]{0:T(1024)} async-done(((f32[2654208]{0:T(1024)}), f32[2654208]{0:T(1024)}) %all-reduce.5.cloned.1.call-update) | async-done | bytes 10616848
  387.8 4.9 collective-permute-done
  396.3 58.1 %collective-permute-done.1 = f32[663552]{0:T(1024)S(1)} collective-permute-done((f32[663552]{0:T(1024)S(1)}, f32[663552]{0:T(1024)S(1)}, u32[]{:S(2)}, u32[]{:S(2)}) %collective-permute-start.1) | collective-permute-done | bytes 2654240 | tf_op jit(solution)/shard_map/ppermute | solution.py:26
  454.7 2.5 collective-permute-start.2
  457.2 114.1 %collective-permute-done.2 = f32[663552]{0:T(1024)S(1)} collective-permute-done((f32[663552]{0:T(1024)S(1)}, f32[663552]{0:T(1024)S(1)}, u32[]{:S(2)}, u32[]{:S(2)}) %collective-permute-start.2) | collective-permute-done | bytes 2654240 | tf_op jit(solution)/shard_map/ppermute | solution.py:26
  571.3 2.8 multiply_add_fusion.3
  574.2 106.1 %all-gather.6.cloned.1.call-done = f32[2654208]{0:T(1024)} async-done(((f32[663552]{0:T(1024)}), f32[2654208]{0:T(1024)}) %all-gather.6.cloned.1.call-update) | async-done | bytes 10616848 | tf_op jit(solution)/shard_map/all_gather | solution.py:226
  680.3 9.3 conditional.5
  689.6 2.1 constant_dynamic-update-slice_fusion.7
  691.7 14.8 %conditional.6 = (f32[442368]{0:T(1024)S(1)}) conditional(s32[]{:T(128)} %convert_element_type.111, () %tuple.39, f32[2654208]{0:T(1024)} %all-gather.6.cloned.1.call-done), branch_computations={%region_23.24_spmd, %region_24.26_spmd} | conditional | flops 14274772992 | bytes 35389476 | solution.py:238
  707.8 15.7 %conditional.7 = (f32[147456]{0:T(1024)S(1)}) conditional(s32[]{:T(128)} %convert_element_type.112, () %tuple.40, f32[2654208]{0:T(1024)} %all-gather.6.cloned.1.call-done), branch_computations={%region_26.27_spmd, %region_27.29_spmd} | conditional | flops 6118096896 | bytes 16515108 | solution.py:238
  724.4 41.5 %conditional.8 = (f32[589824]{0:T(1024)S(1)}) conditional(s32[]{:T(128)} %convert_element_type.112, () %tuple.41, f32[2654208]{0:T(1024)} %all-gather.6.cloned.1.call-done), branch_computations={%region_29.30_spmd, %region_30.32_spmd} | conditional | flops 18353111040 | bytes 44826660 | solution.py:238
  724.4 2.9 multiply_reduce_fusion.3
  728.0 3.2 slice_divide_fusion.3
  731.2 2.4 div.75
  733.7 4.0 fusion.109
  738.9 4.0 convolution_add_fusion.11
  742.9 4.2 fusion.110
  748.4 4.0 convolution_add_fusion.10
  752.4 4.0 fusion.111
  757.7 5.5 fusion.12
  763.2 2.3 reshape.307
  767.5 10.2 conditional.9
  780.6 2.6 fusion.65
  783.2 228.9 %all-reduce.7.cloned.1.call-done = f32[2654208]{0:T(1024)} async-done(((f32[2654208]{0:T(1024)}), f32[2654208]{0:T(1024)}) %all-reduce.7.cloned.1.call-update) | async-done | bytes 10616848
  1012.1 3.5 dynamic-slice_subtract_fusion
  (217 shorter events, 81.5 us)
Async XLA Ops:
  7.2 3.1 copy-start.54
  7.2 47.2 %copy-start.57 = (s32[2]{0:T(128)S(1)}, s32[2]{0:T(128)}, u32[]{:S(2)}) copy-start(s32[2]{0:T(128)} %param.18) | copy-start | bytes 28
  7.2 47.8 %copy-start.3 = (bf16[2,256,384]{2,1,0:T(8,128)(2,1)S(1)}, bf16[2,256,384]{2,1,0:T(8,128)(2,1)}, u32[]{:S(2)}) copy-start(bf16[2,256,384]{2,1,0:T(8,128)(2,1)} %param.16) | copy-start | bytes 1179652
  7.2 68.0 %all-gather.4.cloned.1.call-start = ((), (), s32[]{:S(2)}) async-start(), calls=%async_computation | async-start | bytes 6635520 | tf_op jit(solution)/shard_map/all_gather | solution.py:219
  10.3 375.5 %all-reduce.5.cloned.1.call-start = ((), (), s32[]{:S(2)}) async-start(), calls=%async_computation.2 | async-start | bytes 21233664
  55.0 43.3 %copy-start.45 = (bf16[2,384]{1,0:T(2,128)(2,1)}, bf16[2,384]{1,0:T(2,128)(2,1)S(1)}, u32[]{:S(2)}) copy-start(bf16[2,384]{1,0:T(2,128)(2,1)S(1)} %gather_fusion) | copy-start | bytes 4612
  55.2 44.3 %copy-start.33 = (f32[2,256]{1,0:T(2,128)}, f32[2,256]{1,0:T(2,128)S(1)}, u32[]{:S(2)}) copy-start(f32[2,256]{1,0:T(2,128)S(1)} %broadcast_multiply_fusion.2) | copy-start | bytes 6148
  55.5 25.7 %copy-start.41 = (f32[2,256]{1,0:T(2,128)}, f32[2,256]{1,0:T(2,128)S(1)}, u32[]{:S(2)}) copy-start(f32[2,256]{1,0:T(2,128)S(1)} %fusion.69) | copy-start | bytes 6148
  55.5 42.8 %copy-start.51 = (pred[2]{0:T(512)(128)(4,1)}, pred[2]{0:T(512)(128)(4,1)S(1)}, u32[]{:S(2)}) copy-start(pred[2]{0:T(512)(128)(4,1)S(1)} %compare_and_fusion) | copy-start | bytes 10
  55.5 44.0 %copy-start.43 = (f32[2,256]{1,0:T(2,128)}, f32[2,256]{1,0:T(2,128)S(1)}, u32[]{:S(2)}) copy-start(f32[2,256]{1,0:T(2,128)S(1)} %fusion.85) | copy-start | bytes 6148
  90.4 2.2 slice-start
  98.3 3.3 copy-start.14
  99.5 3.5 copy-start.36
  99.5 3.5 copy-start.38
  101.6 1.5 copy-start.15
  105.5 2.9 copy-start.19
  105.5 1.4 copy-start.29
  107.0 1.5 copy-start.25
  107.0 1.5 copy-start.28
  111.2 2.2 copy-start.27
  115.5 2.5 copy-start.13
  115.5 2.5 copy-start.24
  115.6 2.4 copy-start.37
  118.0 4.2 copy-start.31
  127.1 2.5 copy-start.21
  144.6 3.4 copy-start.20
  146.8 1.6 copy-start.18
  147.9 3.6 copy-start.2
  153.1 3.5 copy-start.12
  156.5 1.5 copy-start.32
  156.5 1.5 copy-start.34
  156.5 1.5 copy-start.39
  156.6 1.5 copy-start.44
  158.0 2.6 copy-start.16
  161.4 1.4 copy-start.56
  161.4 1.4 copy-start.55
  161.4 1.4 copy-start.49
  161.4 2.0 copy-start.46
  167.0 4.1 copy-start.9
  171.1 2.7 copy-start.7
  173.8 2.5 copy-start.6
  177.9 502.3 %all-gather.6.cloned.1.call-start = ((), (), s32[]{:S(2)}) async-start(), calls=%async_computation.1 | async-start | bytes 13271040 | tf_op jit(solution)/shard_map/all_gather | solution.py:226
  387.7 5.0 collective-permute-start
  394.7 176.6 %copy-start.22 = (f32[663552]{0:T(1024)S(1)}, f32[663552]{0:T(1024)}, u32[]{:S(2)}) copy-start(f32[663552]{0:T(1024)} %param.20) | copy-start | bytes 7962628
  394.8 59.7 %collective-permute-start.1 = (f32[663552]{0:T(1024)S(1)}, f32[663552]{0:T(1024)S(1)}, u32[]{:S(2)}, u32[]{:S(2)}) collective-permute-start(f32[663552]{0:T(1024)S(1)} %dynamic-slice_add_fusion), channel_id=1, source_target_pairs={{0,2},{1,3},{2,0},{3,1},{4,6},{5,7},{6,4},{7,5},{8,10},{9,11},{10,... | collective-permute-start | bytes 7962632 | tf_op jit(solution)/shard_map/ppermute | solution.py:26
  454.7 116.6 %collective-permute-start.2 = (f32[663552]{0:T(1024)S(1)}, f32[663552]{0:T(1024)S(1)}, u32[]{:S(2)}, u32[]{:S(2)}) collective-permute-start(f32[663552]{0:T(1024)S(1)} %add.253), channel_id=1, source_target_pairs={{0,4},{1,5},{2,6},{3,7},{4,0},{5,1},{6,2},{7,3},{8,12},{9,13},{10,... | collective-permute-start | bytes 7962632 | tf_op jit(solution)/shard_map/ppermute | solution.py:26
  574.1 438.0 %all-reduce.7.cloned.1.call-start = ((), (), s32[]{:S(2)}) async-start(), calls=%async_computation.3 | async-start | bytes 21233664
  779.3 232.8 %copy-start.5 = (f32[663552]{0:T(1024)S(1)}, f32[663552]{0:T(1024)}, u32[]{:S(2)}) copy-start(f32[663552]{0:T(1024)} %param.19) | copy-start | bytes 7962628
  (16 other events, 15.9 us)
Sparse Core Ops, SparseCore 0:
  10.4 64.7 all-gather.3
  178.1 207.6 all-reduce.4
  574.3 105.9 all-gather.5
  779.4 232.6 all-reduce.6
